TPU v7x, 32 devices: a whole 2x2x4 slice. The times are simulated.
32 devices in a mesh: tm: 4 (over x, core), pair: 8 (over z, y).
Axes of the slice: x: 2, y: 2, z: 4, core: 2. Of those that a mesh axis runs over, the one named last changes fastest.
Arguments:
- orbitals: bfloat16 [8192, 512], P('pair', 'tm'), may hold values from -1.5 to 1.5
- level_gap: float32 [512], replicated, may hold values from 0.05 to 1.5
- screened: bfloat16 [8, 32, 1024, 1024], P('tm', 'pair'), may hold values from -0.008972168 to 0.008972168
- pair_blocks: int32 [32, 2], P('pair'), may hold values from 0 to 7, as said below
Outputs:
- self_energy: float32 [8, 512, 512], P('tm', 'pair')
Inputs may be any that keep to these rules, and one draw needn't show every extreme that they name: `pair_blocks`: each row names two point blocks a <= c; no unordered pair appears in two rows; the pair (0, 7) appears in every draw.
All inputs are finite; a program needn't handle non-finite values.
Results may differ from a plain program's by a relative error of at most 0.0049.
Values may be sent and summed in bfloat16 or wider, within the bound.
A program may use at most 128 MiB of HBM per device.

v0:
```python
import jax
import jax.numpy as jnp
from jax import lax
from jax.sharding import PartitionSpec as P

NOCC = 128


def shards(orbitals, level_gap, screened, pair_blocks):
    block_rows = orbitals.shape[0]
    wanted = pair_blocks.reshape(-1)
    narrow = lax.all_gather(orbitals, "pair", axis=0, tiled=True)
    picked = jnp.take(narrow.reshape(-1, block_rows, narrow.shape[1]), wanted, axis=0)
    chosen = lax.all_gather(picked, "tm", axis=2, tiled=True)
    orbital_count = chosen.shape[2]
    time_local = screened.shape[0]
    pair_local = screened.shape[1]
    time_total = time_local * lax.axis_size("tm")
    first_time = lax.axis_index("tm") * time_local
    moments = (first_time + jnp.arange(time_local)).astype(jnp.float32)
    tau = 6.0 * (moments + 0.5) / time_total
    signs = jnp.where(jnp.arange(orbital_count) < NOCC, 1.0, -1.0).astype(jnp.float32)
    factors = signs[None, :] * jnp.exp(-level_gap[None, :] * tau[:, None])
    totals = []
    for time_step in range(time_local):
        total = jnp.zeros((orbital_count, orbital_count), jnp.float32)
        for pair_step in range(pair_local):
            left = chosen[2 * pair_step]
            right = chosen[2 * pair_step + 1]
            scaled = (left.astype(jnp.float32) * factors[time_step][None, :]).astype(jnp.bfloat16)
            green = lax.dot_general(
                scaled, right, (((1,), (1,)), ((), ())), preferred_element_type=jnp.float32
            )
            product = (green * screened[time_step, pair_step].astype(jnp.float32)).astype(
                jnp.bfloat16
            )
            half = lax.dot_general(
                left, product, (((0,), (0,)), ((), ())), preferred_element_type=jnp.float32
            ).astype(jnp.bfloat16)
            block = jnp.dot(half, right, preferred_element_type=jnp.float32)
            weight = jnp.where(
                pair_blocks[pair_step, 0] == pair_blocks[pair_step, 1], 0.5, 1.0
            ).astype(jnp.float32)
            total = total + weight * (block + block.T)
        totals.append(total)
    partial_sum = jnp.stack(totals, axis=0)
    return lax.psum_scatter(partial_sum, "pair", scatter_dimension=1, tiled=True)


def solution(mesh):
    return jax.shard_map(
        shards,
        mesh=mesh,
        in_specs=(P("pair", "tm"), P(), P("tm", "pair", None, None), P("pair", None)),
        out_specs=P("tm", "pair", None),
        check_vma=False,
    )
```

profile of v0, /device:TPU:0, one launch (start us, length us, event | category | flops | bytes accessed | tf_op | source)
XLA Modules:
  0.0 293.7 jit_solution(13461157398110118424)
XLA Ops:
  6.5 0.0 all-gather.3.cloned.1.call-start
  6.5 0.7 all-gather.3.cloned.1.call-update
  7.3 0.0 all-gather.5.cloned.1.call-start
  7.3 0.8 copy.15
  8.1 0.1 reshape.146
  8.2 0.1 reshape.144
  8.3 53.0 %all-gather.3.cloned.1.call-done = bf16[8192,128]{1,0:T(8,128)(2,1)} async-done(((bf16[1024,128]{1,0:T(8,128)(2,1)}), bf16[8192,128]{1,0:T(8,128)(2,1)}) %all-gather.3.cloned.1.call-update) | async-done | bytes 2097168 | tf_op jit(solution)/shard_map/all_gather | solution.py:12
  61.3 2.5 gather_fusion
  63.8 0.0 copy-start.9
  63.9 0.0 copy-start.8
  63.9 1.7 broadcast_select_fusion
  65.5 0.0 all-gather.5.cloned.1.call-update
  65.5 0.0 reduce-scatter.2.cloned.1.call-start
  65.6 0.0 copy-done.9
  65.6 0.0 copy-done.8
  65.6 0.7 fusion.115
  71.3 0.1 exponential_multiply_fusion
  71.4 52.2 %all-gather.5.cloned.1.call-done = bf16[8,1024,512]{2,1,0:T(8,128)(2,1)} async-done(((bf16[8,1024,128]{2,1,0:T(8,128)(2,1)}), bf16[8,1024,512]{2,1,0:T(8,128)(2,1)}) %all-gather.5.cloned.1.call-update) | async-done | bytes 8388624 | tf_op jit(solution)/shard_map/all_gather | solution.py:14
  123.6 4.9 %convolution_convert_fusion.3 = bf16[512,1024]{1,0:T(8,128)(2,1)S(1)} fusion(bf16[2,4,1024,1024]{3,2,1,0:T(8,128)(2,1)} %param.6, f32[512]{0:T(512)S(1)} %bitcast.218, bf16[8,1024,512]{2,1,0:T(8,128)(2,1)} %all-gather.5.cloned.1.call-done), kind=kOutput, calls=%fused_computation.38 | convolution fusion | flops 2152726528 | bytes 6293504 | tf_op jit(solution)/shard_map/dot_general | solution.py:37
  128.5 1.9 fusion.104
  130.5 0.3 copy.21
  130.8 6.0 %convolution_convert_fusion.2 = bf16[512,1024]{1,0:T(8,128)(2,1)} fusion(bf16[2,4,1024,1024]{3,2,1,0:T(8,128)(2,1)} %param.6, f32[512]{0:T(512)S(1)} %bitcast.219, bf16[8,1024,512]{2,1,0:T(8,128)(2,1)} %all-gather.5.cloned.1.call-done), kind=kOutput, calls=%fused_computation.37 | convolution fusion | flops 2152726528 | bytes 6293504 | tf_op jit(solution)/shard_map/dot_general | solution.py:37
  136.8 2.2 fusion.106
  139.0 1.4 copy.22
  140.4 5.9 %convolution_convert_fusion = bf16[512,1024]{1,0:T(8,128)(2,1)} fusion(bf16[2,4,1024,1024]{3,2,1,0:T(8,128)(2,1)} %param.6, f32[512]{0:T(512)S(1)} %bitcast.220, bf16[8,1024,512]{2,1,0:T(8,128)(2,1)} %all-gather.5.cloned.1.call-done), kind=kOutput, calls=%fused_computation.35 | convolution fusion | flops 2152726528 | bytes 6293504 | tf_op jit(solution)/shard_map/dot_general | solution.py:37
  146.3 3.2 %fusion.110 = f32[512,512]{1,0:T(8,128)} fusion(bf16[512,1024]{1,0:T(8,128)(2,1)} %convolution_convert_fusion, bf16[8,1024,512]{2,1,0:T(8,128)(2,1)} %all-gather.5.cloned.1.call-done), kind=kOutput, calls=%fused_computation.109 | convolution fusion | flops 536870912 | bytes 3145728 | tf_op jit(solution)/shard_map/dot_general | solution.py:40
  149.6 2.5 copy.24
  152.1 6.0 %convolution_convert_fusion.1 = bf16[512,1024]{1,0:T(8,128)(2,1)} fusion(bf16[2,4,1024,1024]{3,2,1,0:T(8,128)(2,1)} %param.6, f32[512]{0:T(512)S(1)} %bitcast.221, bf16[8,1024,512]{2,1,0:T(8,128)(2,1)} %all-gather.5.cloned.1.call-done), kind=kOutput, calls=%fused_computation.36 | convolution fusion | flops 2152726528 | bytes 6293504 | tf_op jit(solution)/shard_map/dot_general | solution.py:37
  158.1 3.2 %fusion.108 = f32[512,512]{1,0:T(8,128)} fusion(bf16[512,1024]{1,0:T(8,128)(2,1)} %convolution_convert_fusion.1, bf16[8,1024,512]{2,1,0:T(8,128)(2,1)} %all-gather.5.cloned.1.call-done), kind=kOutput, calls=%fused_computation.107 | convolution fusion | flops 536870912 | bytes 3145728 | tf_op jit(solution)/shard_map/dot_general | solution.py:40
  161.3 2.6 copy.23
  163.9 6.1 %convolution_convert_fusion.4 = bf16[512,1024]{1,0:T(8,128)(2,1)} fusion(bf16[2,4,1024,1024]{3,2,1,0:T(8,128)(2,1)} %param.6, f32[512]{0:T(512)S(1)} %bitcast.214, bf16[8,1024,512]{2,1,0:T(8,128)(2,1)} %all-gather.5.cloned.1.call-done), kind=kOutput, calls=%fused_computation.39 | convolution fusion | flops 2152726528 | bytes 6293504 | tf_op jit(solution)/shard_map/dot_general | solution.py:37
  170.0 3.2 %fusion.111 = f32[512,512]{1,0:T(8,128)} fusion(bf16[512,1024]{1,0:T(8,128)(2,1)} %convolution_convert_fusion.4, bf16[8,1024,512]{2,1,0:T(8,128)(2,1)} %all-gather.5.cloned.1.call-done), kind=kOutput, calls=%fused_computation.110 | convolution fusion | flops 536870912 | bytes 3145728 | tf_op jit(solution)/shard_map/dot_general | solution.py:40
  173.2 2.5 copy.20
  175.7 5.9 %convolution_convert_fusion.5 = bf16[512,1024]{1,0:T(8,128)(2,1)} fusion(bf16[2,4,1024,1024]{3,2,1,0:T(8,128)(2,1)} %param.6, f32[512]{0:T(512)S(1)} %bitcast.215, bf16[8,1024,512]{2,1,0:T(8,128)(2,1)} %all-gather.5.cloned.1.call-done), kind=kOutput, calls=%fused_computation.40 | convolution fusion | flops 2152726528 | bytes 6293504 | tf_op jit(solution)/shard_map/dot_general | solution.py:37
  181.7 3.2 %fusion.109 = f32[512,512]{1,0:T(8,128)} fusion(bf16[512,1024]{1,0:T(8,128)(2,1)} %convolution_convert_fusion.5, bf16[8,1024,512]{2,1,0:T(8,128)(2,1)} %all-gather.5.cloned.1.call-done), kind=kOutput, calls=%fused_computation.108 | convolution fusion | flops 536870912 | bytes 3145728 | tf_op jit(solution)/shard_map/dot_general | solution.py:40
  184.9 2.5 copy.19
  187.4 5.9 %convolution_convert_fusion.7 = bf16[512,1024]{1,0:T(8,128)(2,1)} fusion(bf16[2,4,1024,1024]{3,2,1,0:T(8,128)(2,1)} %param.6, f32[512]{0:T(512)S(1)} %bitcast.216, bf16[8,1024,512]{2,1,0:T(8,128)(2,1)} %all-gather.5.cloned.1.call-done), kind=kOutput, calls=%fused_computation.42 | convolution fusion | flops 2152726528 | bytes 6293504 | tf_op jit(solution)/shard_map/dot_general | solution.py:37
  193.3 3.2 %fusion.105 = f32[512,512]{1,0:T(8,128)} fusion(bf16[512,1024]{1,0:T(8,128)(2,1)} %convolution_convert_fusion.7, bf16[8,1024,512]{2,1,0:T(8,128)(2,1)} %all-gather.5.cloned.1.call-done), kind=kOutput, calls=%fused_computation.104 | convolution fusion | flops 536870912 | bytes 3145728 | tf_op jit(solution)/shard_map/dot_general | solution.py:40
  196.6 2.5 copy.17
  199.1 5.9 %convolution_convert_fusion.6 = bf16[512,1024]{1,0:T(8,128)(2,1)} fusion(bf16[2,4,1024,1024]{3,2,1,0:T(8,128)(2,1)} %param.6, f32[512]{0:T(512)S(1)} %bitcast.217, bf16[8,1024,512]{2,1,0:T(8,128)(2,1)} %all-gather.5.cloned.1.call-done), kind=kOutput, calls=%fused_computation.41 | convolution fusion | flops 2152726528 | bytes 6293504 | tf_op jit(solution)/shard_map/dot_general | solution.py:37
  205.0 3.3 %fusion.107 = f32[512,512]{1,0:T(8,128)} fusion(bf16[512,1024]{1,0:T(8,128)(2,1)} %convolution_convert_fusion.6, bf16[8,1024,512]{2,1,0:T(8,128)(2,1)} %all-gather.5.cloned.1.call-done), kind=kOutput, calls=%fused_computation.106 | convolution fusion | flops 536870912 | bytes 3145728 | tf_op jit(solution)/shard_map/dot_general | solution.py:40
  208.3 2.5 copy.18
  210.8 0.0 copy-start
  210.8 0.0 copy-start.1
  210.8 0.0 copy-start.2
  210.8 0.0 copy-start.3
  210.8 0.0 copy-start.4
  210.8 0.0 copy-start.5
  210.8 0.0 copy-start.6
  210.8 0.0 copy-start.7
  210.8 3.7 %fusion.34 = f32[1,512,512]{2,1,0:T(8,128)S(1)} fusion(f32[512,512]{1,0:T(8,128)} %fusion.110, f32[512,512]{0,1:T(8,128)} %copy.24, f32[512,512]{1,0:T(8,128)} %fusion.108, f32[512,512]{0,1:T(8,128)} %copy.23, f32[512,512]{1,0:T(8,128)S(1)} %fusion.106, f32[512,512]{0,1:T(8,128)} %copy.22, f32[512,512]{1,0:T(8,128)S(1)} %fusion.104, ...), kind=kLoop, calls=%fused_computation.58 | loop fusion | flops 2883584 | bytes 9437200 | tf_op jit(solution)/shard_map/stack | solution.py:46
  214.6 0.0 copy-done
  214.6 0.0 copy-done.1
  214.6 0.0 copy-done.2
  214.6 0.0 copy-done.3
  214.6 0.2 copy-done.4
  214.9 0.3 copy-done.5
  215.2 0.3 copy-done.6
  215.5 0.3 copy-done.7
  215.8 1.0 fusion.42
  216.8 1.5 pad_maximum_fusion
  218.3 0.0 reduce-scatter.2.cloned.1.call-update
  218.3 68.9 %reduce-scatter.2.cloned.1.call-done = f32[2,64,512]{2,1,0:T(8,128)} async-done(((f32[2,512,512]{2,1,0:T(8,128)}), f32[2,64,512]{2,1,0:T(8,128)}) %reduce-scatter.2.cloned.1.call-update) | async-done | bytes 262160 | tf_op jit(solution)/shard_map/reduce_scatter | solution.py:47
  (7 shorter events, 0.0 us)
Async XLA Ops:
  6.5 54.8 %all-gather.3.cloned.1.call-start = ((), (), s32[]{:S(2)}) async-start(), calls=%async_computation.1 | async-start | bytes 2359296 | tf_op jit(solution)/shard_map/all_gather | solution.py:12
  7.3 116.4 %all-gather.5.cloned.1.call-start = ((), (), s32[]{:S(2)}) async-start(), calls=%async_computation.2 | async-start | bytes 10485760 | tf_op jit(solution)/shard_map/all_gather | solution.py:14
  63.8 1.8 copy-start.9
  63.9 1.8 copy-start.8
  65.5 221.7 %reduce-scatter.2.cloned.1.call-start = ((), (), s32[]{:S(2)}) async-start(), calls=%async_computation.3 | async-start | bytes 2359296 | tf_op jit(solution)/shard_map/reduce_scatter | solution.py:47
  210.8 3.8 %copy-start = (f32[512,512]{1,0:T(8,128)S(1)}, f32[512,512]{1,0:T(8,128)}, u32[]{:S(2)}) copy-start(f32[512,512]{1,0:T(8,128)} %fusion.111) | copy-start | bytes 3145732
  210.8 3.8 %copy-start.1 = (f32[512,512]{0,1:T(8,128)S(1)}, f32[512,512]{0,1:T(8,128)}, u32[]{:S(2)}) copy-start(f32[512,512]{0,1:T(8,128)} %copy.20) | copy-start | bytes 3145732
  210.8 3.8 %copy-start.2 = (f32[512,512]{1,0:T(8,128)S(1)}, f32[512,512]{1,0:T(8,128)}, u32[]{:S(2)}) copy-start(f32[512,512]{1,0:T(8,128)} %fusion.109) | copy-start | bytes 3145732
  210.8 3.8 %copy-start.3 = (f32[512,512]{0,1:T(8,128)S(1)}, f32[512,512]{0,1:T(8,128)}, u32[]{:S(2)}) copy-start(f32[512,512]{0,1:T(8,128)} %copy.19) | copy-start | bytes 3145732
  210.8 4.1 %copy-start.4 = (f32[512,512]{1,0:T(8,128)S(1)}, f32[512,512]{1,0:T(8,128)}, u32[]{:S(2)}) copy-start(f32[512,512]{1,0:T(8,128)} %fusion.105) | copy-start | bytes 3145732
  210.8 4.4 %copy-start.5 = (f32[512,512]{0,1:T(8,128)S(1)}, f32[512,512]{0,1:T(8,128)}, u32[]{:S(2)}) copy-start(f32[512,512]{0,1:T(8,128)} %copy.17) | copy-start | bytes 3145732
  210.8 4.7 %copy-start.6 = (f32[512,512]{1,0:T(8,128)S(1)}, f32[512,512]{1,0:T(8,128)}, u32[]{:S(2)}) copy-start(f32[512,512]{1,0:T(8,128)} %fusion.107) | copy-start | bytes 3145732
  210.8 4.9 %copy-start.7 = (f32[512,512]{0,1:T(8,128)S(1)}, f32[512,512]{0,1:T(8,128)}, u32[]{:S(2)}) copy-start(f32[512,512]{0,1:T(8,128)} %copy.18) | copy-start | bytes 3145732
Sparse Core Ops, SparseCore 0:
  9.5 51.7 all-gather.2
  65.7 57.8 all-gather.4
  218.5 68.6 reduce-scatter.1
where the time goes:
time: 294 us
  waiting for transfers between devices  175 us (60%)
  matrix products  70.1 us (24%)
  local copies, waits for them, and re-layouts  22.4 us (8%)
  between operations  18.3 us (6%)
  other arithmetic  8.04 us (3%)
    reduce_scatter x1, waiting for transfers between devices, shards(): lax.psum_scatter(partial_sum, 'pair', scatter_dimension=1, tiled=True)  68.9 us
    all_gather x1, waiting for transfers between devices, shards(): narrow = lax.all_gather(orbitals, 'pair', axis=0, tiled=True)  53 us
    all_gather x1, waiting for transfers between devices, shards(): chosen = lax.all_gather(picked, 'tm', axis=2, tiled=True)  52.2 us
    dot_general x8, matrix products, shards(): lax.dot_general(left, product, (((0,), (0,)), ((), ())), preferred_elemen...  46.5 us
    dot_general x8, matrix products, shards(): block = jnp.dot(half, right, preferred_element_type=jnp.float32)  23.6 us
    dot_general x8, local copies, waits for them, and re-layouts, shards(): block = jnp.dot(half, right, preferred_element_type=jnp.float32)  17 us
    another operation x3, other arithmetic, shards(): partial_sum = jnp.stack(totals, axis=0)  6.27 us
  transfers between devices with their start and end apart: 3, of which 3 were waited for; matrix products, arithmetic and copies ran while one was open for 1% of the time, Pallas kernels for 0%

commit v1 on v0

--- a/solution.py
+++ b/solution.py
@@ -9,7 +9,12 @@
 def shards(orbitals, level_gap, screened, pair_blocks):
     block_rows = orbitals.shape[0]
     wanted = pair_blocks.reshape(-1)
-    narrow = lax.all_gather(orbitals, "pair", axis=0, tiled=True)
+    ring = [orbitals]
+    for hop in range(7):
+        ring.append(lax.ppermute(ring[-1], "pair", [(dev, (dev + 1) % 8) for dev in range(8)]))
+    narrow = jnp.roll(
+        jnp.concatenate(ring[::-1], axis=0), (lax.axis_index("pair") + 1) * ring[0].shape[0], axis=0
+    )
     picked = jnp.take(narrow.reshape(-1, block_rows, narrow.shape[1]), wanted, axis=0)
     chosen = lax.all_gather(picked, "tm", axis=2, tiled=True)
     orbital_count = chosen.shape[2]

time: 294 us -> 311 us (1.058)
  waiting for transfers between devices: 175 us -> 185 us
  starting transfers between devices: 0.08 us -> 3.24 us
    ppermute x0 -> x7, waiting for transfers between devices: none -> 65 us  [shards(): lax.ppermute(ring[-1], 'pair', [(dev, (dev + 1) % 8) for dev in range(8)])]
    all_gather x1 -> x0, waiting for transfers between devices: 53 us -> none  [shards(): narrow = lax.all_gather(orbitals, 'pair', axis=0, tiled=True)]
  transfers between devices with their start and end apart: 3 -> 9, of which waited for: 3 -> 9; matrix products, arithmetic and copies ran while one was open for 1% -> 1% of each run, Pallas kernels for 0% -> 0%
where the time goes in v1:
time: 311 us; the launch traced here: 310 us
  waiting for transfers between devices  185 us (59%)
  matrix products  70.2 us (23%)
  local copies, waits for them, and re-layouts  23.7 us (8%)
  between operations  18.8 us (6%)
  other arithmetic  9.65 us (3%)
  starting transfers between devices  3.24 us (1%)
    reduce_scatter x1, waiting for transfers between devices, shards(): lax.psum_scatter(partial_sum, 'pair', scatter_dimension=1, tiled=True)  68.9 us
    ppermute x7, waiting for transfers between devices, shards(): lax.ppermute(ring[-1], 'pair', [(dev, (dev + 1) % 8) for dev in range(8)])  65 us
    all_gather x1, waiting for transfers between devices, shards(): chosen = lax.all_gather(picked, 'tm', axis=2, tiled=True)  50.6 us
    dot_general x8, matrix products, shards(): lax.dot_general(left, product, (((0,), (0,)), ((), ())), preferred_elemen...  46.6 us
    dot_general x8, matrix products, shards(): block = jnp.dot(half, right, preferred_element_type=jnp.float32)  23.5 us
    dot_general x8, local copies, waits for them, and re-layouts, shards(): block = jnp.dot(half, right, preferred_element_type=jnp.float32)  17.1 us
    another operation x3, other arithmetic, shards(): partial_sum = jnp.stack(totals, axis=0)  6.26 us
  transfers between devices with their start and end apart: 9, of which 9 were waited for; matrix products, arithmetic and copies ran while one was open for 1% of the time, Pallas kernels for 0%

profile of v1, /device:TPU:0, one launch (start us, length us, event | category | flops | bytes accessed | tf_op | source)
XLA Modules:
  0.0 310.1 jit_solution(5586169564269264432)
XLA Ops:
  6.5 0.0 all-gather.2.cloned.1.call-start
  6.5 3.0 collective-permute-start
  9.5 9.6 %collective-permute-done = bf16[1024,128]{1,0:T(8,128)(2,1)S(1)} collective-permute-done((bf16[1024,128]{1,0:T(8,128)(2,1)}, bf16[1024,128]{1,0:T(8,128)(2,1)S(1)}, u32[]{:S(2)}, u32[]{:S(2)}) %collective-permute-start) | collective-permute-done | bytes 262176 | tf_op jit(solution)/shard_map/ppermute | solution.py:14
  19.2 0.0 collective-permute-start.1
  19.2 10.2 %collective-permute-done.1 = bf16[1024,128]{1,0:T(8,128)(2,1)S(1)} collective-permute-done((bf16[1024,128]{1,0:T(8,128)(2,1)S(1)}, bf16[1024,128]{1,0:T(8,128)(2,1)S(1)}, u32[]{:S(2)}, u32[]{:S(2)}) %collective-permute-start.1) | collective-permute-done | bytes 262176 | tf_op jit(solution)/shard_map/ppermute | solution.py:14
  29.3 0.0 collective-permute-start.2
  29.3 9.3 %collective-permute-done.2 = bf16[1024,128]{1,0:T(8,128)(2,1)S(1)} collective-permute-done((bf16[1024,128]{1,0:T(8,128)(2,1)S(1)}, bf16[1024,128]{1,0:T(8,128)(2,1)S(1)}, u32[]{:S(2)}, u32[]{:S(2)}) %collective-permute-start.2) | collective-permute-done | bytes 262176 | tf_op jit(solution)/shard_map/ppermute | solution.py:14
  38.6 0.0 collective-permute-start.3
  38.6 9.1 %collective-permute-done.3 = bf16[1024,128]{1,0:T(8,128)(2,1)S(1)} collective-permute-done((bf16[1024,128]{1,0:T(8,128)(2,1)S(1)}, bf16[1024,128]{1,0:T(8,128)(2,1)S(1)}, u32[]{:S(2)}, u32[]{:S(2)}) %collective-permute-start.3) | collective-permute-done | bytes 262176 | tf_op jit(solution)/shard_map/ppermute | solution.py:14
  47.7 0.0 collective-permute-start.4
  47.7 9.1 %collective-permute-done.4 = bf16[1024,128]{1,0:T(8,128)(2,1)S(1)} collective-permute-done((bf16[1024,128]{1,0:T(8,128)(2,1)S(1)}, bf16[1024,128]{1,0:T(8,128)(2,1)S(1)}, u32[]{:S(2)}, u32[]{:S(2)}) %collective-permute-start.4) | collective-permute-done | bytes 262176 | tf_op jit(solution)/shard_map/ppermute | solution.py:14
  56.8 0.0 collective-permute-start.5
  56.8 0.8 copy.15
  57.5 0.1 reshape.146
  57.6 8.8 %collective-permute-done.5 = bf16[1024,128]{1,0:T(8,128)(2,1)S(1)} collective-permute-done((bf16[1024,128]{1,0:T(8,128)(2,1)S(1)}, bf16[1024,128]{1,0:T(8,128)(2,1)S(1)}, u32[]{:S(2)}, u32[]{:S(2)}) %collective-permute-start.5) | collective-permute-done | bytes 262176 | tf_op jit(solution)/shard_map/ppermute | solution.py:14
  66.5 0.0 collective-permute-start.6
  66.5 0.1 reshape.144
  66.6 9.0 %collective-permute-done.6 = bf16[1024,128]{1,0:T(8,128)(2,1)S(1)} collective-permute-done((bf16[1024,128]{1,0:T(8,128)(2,1)S(1)}, bf16[1024,128]{1,0:T(8,128)(2,1)S(1)}, u32[]{:S(2)}, u32[]{:S(2)}) %collective-permute-start.6) | collective-permute-done | bytes 262176 | tf_op jit(solution)/shard_map/ppermute | solution.py:14
  75.8 1.0 constant_dynamic-update-slice_fusion.8
  77.1 0.0 copy-done.8
  77.2 0.1 constant_dynamic-slice_fusion
  77.3 2.2 gather_fusion
  79.5 3.3 %broadcast_select_fusion = bf16[8,1024,128]{2,1,0:T(8,128)(2,1)} fusion(bf16[8,1024,128]{2,1,0:T(8,128)(2,1)} %gather_fusion, pred[8]{0:T(512)(128)(4,1)S(1)} %compare_and_fusion), kind=kLoop, calls=%fused_computation.34 | loop fusion | flops 1048576 | bytes 4194312 | tf_op jit(solution)/shard_map/jit(_take)/select_n | solution.py:18
  82.8 0.0 all-gather.2.cloned.1.call-update
  82.8 0.2 reduce-scatter.2.cloned.1.call-start
  83.1 0.0 copy-done.10
  83.1 0.0 copy-done.9
  83.1 0.7 fusion.115
  88.8 0.1 exponential_multiply_fusion
  88.9 50.6 %all-gather.2.cloned.1.call-done = bf16[8,1024,512]{2,1,0:T(8,128)(2,1)} async-done(((bf16[8,1024,128]{2,1,0:T(8,128)(2,1)}), bf16[8,1024,512]{2,1,0:T(8,128)(2,1)}) %all-gather.2.cloned.1.call-update) | async-done | bytes 8388624 | tf_op jit(solution)/shard_map/all_gather | solution.py:19
  139.5 4.9 %convolution_convert_fusion.3 = bf16[512,1024]{1,0:T(8,128)(2,1)S(1)} fusion(bf16[2,4,1024,1024]{3,2,1,0:T(8,128)(2,1)} %param.6, f32[512]{0:T(512)S(1)} %bitcast.218, bf16[8,1024,512]{2,1,0:T(8,128)(2,1)} %all-gather.2.cloned.1.call-done), kind=kOutput, calls=%fused_computation.38 | convolution fusion | flops 2152726528 | bytes 6293504 | tf_op jit(solution)/shard_map/dot_general | solution.py:42
  144.4 1.9 fusion.104
  146.4 0.3 copy.21
  146.7 6.0 %convolution_convert_fusion.2 = bf16[512,1024]{1,0:T(8,128)(2,1)} fusion(bf16[2,4,1024,1024]{3,2,1,0:T(8,128)(2,1)} %param.6, f32[512]{0:T(512)S(1)} %bitcast.219, bf16[8,1024,512]{2,1,0:T(8,128)(2,1)} %all-gather.2.cloned.1.call-done), kind=kOutput, calls=%fused_computation.37 | convolution fusion | flops 2152726528 | bytes 6293504 | tf_op jit(solution)/shard_map/dot_general | solution.py:42
  152.7 2.2 fusion.106
  155.0 1.4 copy.22
  156.3 5.9 %convolution_convert_fusion = bf16[512,1024]{1,0:T(8,128)(2,1)} fusion(bf16[2,4,1024,1024]{3,2,1,0:T(8,128)(2,1)} %param.6, f32[512]{0:T(512)S(1)} %bitcast.220, bf16[8,1024,512]{2,1,0:T(8,128)(2,1)} %all-gather.2.cloned.1.call-done), kind=kOutput, calls=%fused_computation.35 | convolution fusion | flops 2152726528 | bytes 6293504 | tf_op jit(solution)/shard_map/dot_general | solution.py:42
  162.2 3.3 %fusion.110 = f32[512,512]{1,0:T(8,128)} fusion(bf16[512,1024]{1,0:T(8,128)(2,1)} %convolution_convert_fusion, bf16[8,1024,512]{2,1,0:T(8,128)(2,1)} %all-gather.2.cloned.1.call-done), kind=kOutput, calls=%fused_computation.109 | convolution fusion | flops 536870912 | bytes 3145728 | tf_op jit(solution)/shard_map/dot_general | solution.py:45
  165.5 2.5 copy.24
  168.0 6.0 %convolution_convert_fusion.1 = bf16[512,1024]{1,0:T(8,128)(2,1)} fusion(bf16[2,4,1024,1024]{3,2,1,0:T(8,128)(2,1)} %param.6, f32[512]{0:T(512)S(1)} %bitcast.221, bf16[8,1024,512]{2,1,0:T(8,128)(2,1)} %all-gather.2.cloned.1.call-done), kind=kOutput, calls=%fused_computation.36 | convolution fusion | flops 2152726528 | bytes 6293504 | tf_op jit(solution)/shard_map/dot_general | solution.py:42
  174.0 3.2 %fusion.108 = f32[512,512]{1,0:T(8,128)} fusion(bf16[512,1024]{1,0:T(8,128)(2,1)} %convolution_convert_fusion.1, bf16[8,1024,512]{2,1,0:T(8,128)(2,1)} %all-gather.2.cloned.1.call-done), kind=kOutput, calls=%fused_computation.107 | convolution fusion | flops 536870912 | bytes 3145728 | tf_op jit(solution)/shard_map/dot_general | solution.py:45
  177.2 2.6 copy.23
  179.8 6.1 %convolution_convert_fusion.4 = bf16[512,1024]{1,0:T(8,128)(2,1)} fusion(bf16[2,4,1024,1024]{3,2,1,0:T(8,128)(2,1)} %param.6, f32[512]{0:T(512)S(1)} %bitcast.214, bf16[8,1024,512]{2,1,0:T(8,128)(2,1)} %all-gather.2.cloned.1.call-done), kind=kOutput, calls=%fused_computation.39 | convolution fusion | flops 2152726528 | bytes 6293504 | tf_op jit(solution)/shard_map/dot_general | solution.py:42
  186.0 3.2 %fusion.111 = f32[512,512]{1,0:T(8,128)} fusion(bf16[512,1024]{1,0:T(8,128)(2,1)} %convolution_convert_fusion.4, bf16[8,1024,512]{2,1,0:T(8,128)(2,1)} %all-gather.2.cloned.1.call-done), kind=kOutput, calls=%fused_computation.110 | convolution fusion | flops 536870912 | bytes 3145728 | tf_op jit(solution)/shard_map/dot_general | solution.py:45
  189.2 2.6 copy.20
  191.8 5.9 %convolution_convert_fusion.5 = bf16[512,1024]{1,0:T(8,128)(2,1)} fusion(bf16[2,4,1024,1024]{3,2,1,0:T(8,128)(2,1)} %param.6, f32[512]{0:T(512)S(1)} %bitcast.215, bf16[8,1024,512]{2,1,0:T(8,128)(2,1)} %all-gather.2.cloned.1.call-done), kind=kOutput, calls=%fused_computation.40 | convolution fusion | flops 2152726528 | bytes 6293504 | tf_op jit(solution)/shard_map/dot_general | solution.py:42
  197.7 3.2 %fusion.109 = f32[512,512]{1,0:T(8,128)} fusion(bf16[512,1024]{1,0:T(8,128)(2,1)} %convolution_convert_fusion.5, bf16[8,1024,512]{2,1,0:T(8,128)(2,1)} %all-gather.2.cloned.1.call-done), kind=kOutput, calls=%fused_computation.108 | convolution fusion | flops 536870912 | bytes 3145728 | tf_op jit(solution)/shard_map/dot_general | solution.py:45
  200.9 2.6 copy.19
  203.5 5.9 %convolution_convert_fusion.7 = bf16[512,1024]{1,0:T(8,128)(2,1)} fusion(bf16[2,4,1024,1024]{3,2,1,0:T(8,128)(2,1)} %param.6, f32[512]{0:T(512)S(1)} %bitcast.216, bf16[8,1024,512]{2,1,0:T(8,128)(2,1)} %all-gather.2.cloned.1.call-done), kind=kOutput, calls=%fused_computation.42 | convolution fusion | flops 2152726528 | bytes 6293504 | tf_op jit(solution)/shard_map/dot_general | solution.py:42
  209.4 3.2 %fusion.105 = f32[512,512]{1,0:T(8,128)} fusion(bf16[512,1024]{1,0:T(8,128)(2,1)} %convolution_convert_fusion.7, bf16[8,1024,512]{2,1,0:T(8,128)(2,1)} %all-gather.2.cloned.1.call-done), kind=kOutput, calls=%fused_computation.104 | convolution fusion | flops 536870912 | bytes 3145728 | tf_op jit(solution)/shard_map/dot_general | solution.py:45
  212.6 2.5 copy.17
  215.1 5.9 %convolution_convert_fusion.6 = bf16[512,1024]{1,0:T(8,128)(2,1)} fusion(bf16[2,4,1024,1024]{3,2,1,0:T(8,128)(2,1)} %param.6, f32[512]{0:T(512)S(1)} %bitcast.217, bf16[8,1024,512]{2,1,0:T(8,128)(2,1)} %all-gather.2.cloned.1.call-done), kind=kOutput, calls=%fused_computation.41 | convolution fusion | flops 2152726528 | bytes 6293504 | tf_op jit(solution)/shard_map/dot_general | solution.py:42
  221.0 3.2 %fusion.107 = f32[512,512]{1,0:T(8,128)} fusion(bf16[512,1024]{1,0:T(8,128)(2,1)} %convolution_convert_fusion.6, bf16[8,1024,512]{2,1,0:T(8,128)(2,1)} %all-gather.2.cloned.1.call-done), kind=kOutput, calls=%fused_computation.106 | convolution fusion | flops 536870912 | bytes 3145728 | tf_op jit(solution)/shard_map/dot_general | solution.py:45
  224.3 2.6 copy.18
  226.8 0.0 copy-start.4
  226.9 3.7 %fusion.34 = f32[1,512,512]{2,1,0:T(8,128)S(1)} fusion(f32[512,512]{1,0:T(8,128)} %fusion.110, f32[512,512]{0,1:T(8,128)} %copy.24, f32[512,512]{1,0:T(8,128)} %fusion.108, f32[512,512]{0,1:T(8,128)} %copy.23, f32[512,512]{1,0:T(8,128)S(1)} %fusion.106, f32[512,512]{0,1:T(8,128)} %copy.22, f32[512,512]{1,0:T(8,128)S(1)} %fusion.104, ...), kind=kLoop, calls=%fused_computation.58 | loop fusion | flops 2883584 | bytes 9437200 | tf_op jit(solution)/shard_map/stack | solution.py:51
  230.6 0.2 copy-done.4
  230.9 0.3 copy-done.5
  231.2 0.3 copy-done.6
  231.5 0.3 copy-done.7
  231.8 1.0 fusion.42
  232.8 1.5 pad_maximum_fusion
  234.3 0.0 reduce-scatter.2.cloned.1.call-update
  234.3 68.9 %reduce-scatter.2.cloned.1.call-done = f32[2,64,512]{2,1,0:T(8,128)} async-done(((f32[2,512,512]{2,1,0:T(8,128)}), f32[2,64,512]{2,1,0:T(8,128)}) %reduce-scatter.2.cloned.1.call-update) | async-done | bytes 262160 | tf_op jit(solution)/shard_map/reduce_scatter | solution.py:52
  (36 shorter events, 0.6 us)
Async XLA Ops:
  6.5 70.6 %copy-start.8 = (bf16[1024,128]{1,0:T(8,128)(2,1)S(1)}, bf16[1024,128]{1,0:T(8,128)(2,1)}, u32[]{:S(2)}) copy-start(bf16[1024,128]{1,0:T(8,128)(2,1)} %param.4) | copy-start | bytes 786436
  6.5 133.0 %all-gather.2.cloned.1.call-start = ((), (), s32[]{:S(2)}) async-start(), calls=%async_computation.1 | async-start | bytes 10485760 | tf_op jit(solution)/shard_map/all_gather | solution.py:19
  6.5 12.6 %collective-permute-start = (bf16[1024,128]{1,0:T(8,128)(2,1)}, bf16[1024,128]{1,0:T(8,128)(2,1)S(1)}, u32[]{:S(2)}, u32[]{:S(2)}) collective-permute-start(bf16[1024,128]{1,0:T(8,128)(2,1)} %param.4), channel_id=1, source_target_pairs={{0,1},{1,2},{2,3},{3,4},{4,5},{5,6},{6,7},{7,0},{8,9},{9,10},{10,1... | collective-permute-start | bytes 786440 | tf_op jit(solution)/shard_map/ppermute | solution.py:14
  19.2 10.2 %collective-permute-start.1 = (bf16[1024,128]{1,0:T(8,128)(2,1)S(1)}, bf16[1024,128]{1,0:T(8,128)(2,1)S(1)}, u32[]{:S(2)}, u32[]{:S(2)}) collective-permute-start(bf16[1024,128]{1,0:T(8,128)(2,1)S(1)} %collective-permute-done), channel_id=1, source_target_pairs={{0,1},{1,2},{2,3},{3,4},{4,5},{5,6},{6,7},{7,0},{8,9},{9,10},{10,1... | collective-permute-start | bytes 786440 | tf_op jit(solution)/shard_map/ppermute | solution.py:14
  29.3 9.3 %collective-permute-start.2 = (bf16[1024,128]{1,0:T(8,128)(2,1)S(1)}, bf16[1024,128]{1,0:T(8,128)(2,1)S(1)}, u32[]{:S(2)}, u32[]{:S(2)}) collective-permute-start(bf16[1024,128]{1,0:T(8,128)(2,1)S(1)} %collective-permute-done.1), channel_id=1, source_target_pairs={{0,1},{1,2},{2,3},{3,4},{4,5},{5,6},{6,7},{7,0},{8,9},{9,10},{10,1... | collective-permute-start | bytes 786440 | tf_op jit(solution)/shard_map/ppermute | solution.py:14
  38.6 9.1 %collective-permute-start.3 = (bf16[1024,128]{1,0:T(8,128)(2,1)S(1)}, bf16[1024,128]{1,0:T(8,128)(2,1)S(1)}, u32[]{:S(2)}, u32[]{:S(2)}) collective-permute-start(bf16[1024,128]{1,0:T(8,128)(2,1)S(1)} %collective-permute-done.2), channel_id=1, source_target_pairs={{0,1},{1,2},{2,3},{3,4},{4,5},{5,6},{6,7},{7,0},{8,9},{9,10},{10,1... | collective-permute-start | bytes 786440 | tf_op jit(solution)/shard_map/ppermute | solution.py:14
  47.7 9.1 %collective-permute-start.4 = (bf16[1024,128]{1,0:T(8,128)(2,1)S(1)}, bf16[1024,128]{1,0:T(8,128)(2,1)S(1)}, u32[]{:S(2)}, u32[]{:S(2)}) collective-permute-start(bf16[1024,128]{1,0:T(8,128)(2,1)S(1)} %collective-permute-done.3), channel_id=1, source_target_pairs={{0,1},{1,2},{2,3},{3,4},{4,5},{5,6},{6,7},{7,0},{8,9},{9,10},{10,1... | collective-permute-start | bytes 786440 | tf_op jit(solution)/shard_map/ppermute | solution.py:14
  56.8 9.7 %collective-permute-start.5 = (bf16[1024,128]{1,0:T(8,128)(2,1)S(1)}, bf16[1024,128]{1,0:T(8,128)(2,1)S(1)}, u32[]{:S(2)}, u32[]{:S(2)}) collective-permute-start(bf16[1024,128]{1,0:T(8,128)(2,1)S(1)} %collective-permute-done.4), channel_id=1, source_target_pairs={{0,1},{1,2},{2,3},{3,4},{4,5},{5,6},{6,7},{7,0},{8,9},{9,10},{10,1... | collective-permute-start | bytes 786440 | tf_op jit(solution)/shard_map/ppermute | solution.py:14
  66.5 9.1 %collective-permute-start.6 = (bf16[1024,128]{1,0:T(8,128)(2,1)S(1)}, bf16[1024,128]{1,0:T(8,128)(2,1)S(1)}, u32[]{:S(2)}, u32[]{:S(2)}) collective-permute-start(bf16[1024,128]{1,0:T(8,128)(2,1)S(1)} %collective-permute-done.5), channel_id=1, source_target_pairs={{0,1},{1,2},{2,3},{3,4},{4,5},{5,6},{6,7},{7,0},{8,9},{9,10},{10,1... | collective-permute-start | bytes 786440 | tf_op jit(solution)/shard_map/ppermute | solution.py:14
  79.5 3.5 %copy-start.10 = (f32[512]{0:T(512)S(1)}, f32[512]{0:T(512)}, u32[]{:S(2)}) copy-start(f32[512]{0:T(512)} %param.5) | copy-start | bytes 6148
  79.5 3.6 %copy-start.9 = (s32[4,2]{0,1:T(2,128)S(1)}, s32[4,2]{0,1:T(2,128)}, u32[]{:S(2)}) copy-start(s32[4,2]{0,1:T(2,128)} %param.7) | copy-start | bytes 100
  82.8 220.4 %reduce-scatter.2.cloned.1.call-start = ((), (), s32[]{:S(2)}) async-start(), calls=%async_computation.2 | async-start | bytes 2359296 | tf_op jit(solution)/shard_map/reduce_scatter | solution.py:52
  226.8 3.8 %copy-start = (f32[512,512]{1,0:T(8,128)S(1)}, f32[512,512]{1,0:T(8,128)}, u32[]{:S(2)}) copy-start(f32[512,512]{1,0:T(8,128)} %fusion.111) | copy-start | bytes 3145732
  226.8 3.8 %copy-start.1 = (f32[512,512]{0,1:T(8,128)S(1)}, f32[512,512]{0,1:T(8,128)}, u32[]{:S(2)}) copy-start(f32[512,512]{0,1:T(8,128)} %copy.20) | copy-start | bytes 3145732
  226.8 3.8 %copy-start.2 = (f32[512,512]{1,0:T(8,128)S(1)}, f32[512,512]{1,0:T(8,128)}, u32[]{:S(2)}) copy-start(f32[512,512]{1,0:T(8,128)} %fusion.109) | copy-start | bytes 3145732
  226.8 3.8 %copy-start.3 = (f32[512,512]{0,1:T(8,128)S(1)}, f32[512,512]{0,1:T(8,128)}, u32[]{:S(2)}) copy-start(f32[512,512]{0,1:T(8,128)} %copy.19) | copy-start | bytes 3145732
  226.8 4.1 %copy-start.4 = (f32[512,512]{1,0:T(8,128)S(1)}, f32[512,512]{1,0:T(8,128)}, u32[]{:S(2)}) copy-start(f32[512,512]{1,0:T(8,128)} %fusion.105) | copy-start | bytes 3145732
  226.8 4.4 %copy-start.5 = (f32[512,512]{0,1:T(8,128)S(1)}, f32[512,512]{0,1:T(8,128)}, u32[]{:S(2)}) copy-start(f32[512,512]{0,1:T(8,128)} %copy.17) | copy-start | bytes 3145732
  226.8 4.7 %copy-start.6 = (f32[512,512]{1,0:T(8,128)S(1)}, f32[512,512]{1,0:T(8,128)}, u32[]{:S(2)}) copy-start(f32[512,512]{1,0:T(8,128)} %fusion.107) | copy-start | bytes 3145732
  226.9 4.9 %copy-start.7 = (f32[512,512]{0,1:T(8,128)S(1)}, f32[512,512]{0,1:T(8,128)}, u32[]{:S(2)}) copy-start(f32[512,512]{0,1:T(8,128)} %copy.18) | copy-start | bytes 3145732
Sparse Core Ops, SparseCore 0:
  82.9 56.5 all-gather.1
  234.5 68.7 reduce-scatter.1
